TPU v7x, 32 devices: a whole 2x2x4 slice. The times are simulated.
32 devices in a mesh: rows: 16 (over z, y, x), grp: 2 (over core).
Axes of the slice: x: 2, y: 2, z: 4, core: 2. Of those that a mesh axis runs over, the one named last changes fastest.
Arguments:
- start_basis: bfloat16 [16384, 64], P(('rows', 'grp')), may hold values from -6 to 6
- kernel_blocks: bfloat16 [2944, 256, 256], P(('rows', 'grp')), may hold values from -0.0390625 to 0.0390625
- block_row: int32 [2944], P(('rows', 'grp')), may hold values from 0 to 63, as said below
- block_col: int32 [2944], P(('rows', 'grp')), may hold values from 0 to 63, as said below
- block_count: int32 [32], P(('rows', 'grp')), may hold values from 1 to 92, as said below
Outputs:
- embedding: float32 [16384, 64], P(('rows', 'grp'))
- projected: float32 [64, 64], replicated
Inputs may be any that keep to these rules, and one draw needn't show every extreme that they name: block_count[d] is the number of live slots of device d, its first ones; device 0 has all 92 live and the last device has 3. `block_row`: each slot's row block is one of its own device's 2 row blocks. `block_col`: each slot's column block is at least its row block; among one device's live slots at most 3 have their column block on any one device, the last device's live slots all lie on itself, and device 0 has a live slot whose column block lies on the last device.
All inputs are finite; a program needn't handle non-finite values.
Results may differ from a plain program's by a relative error of at most 0.0034.
Values may be sent and summed in bfloat16 or wider, within the bound.
A program may use at most 128 MiB of HBM per device.

v0:
```python
import jax
import jax.numpy as jnp
from jax import lax
from jax.sharding import PartitionSpec as P

ITERS = 2


def onehot(index, count, dtype):
    return (index[:, None] == jnp.arange(count, dtype=jnp.int32)[None, :]).astype(dtype)


def on_device(start_basis, kernel_blocks, block_row, block_col, block_count):
    devices = lax.axis_size(("rows", "grp"))
    my_index = lax.axis_index(("rows", "grp"))
    block_size = kernel_blocks.shape[1]
    columns = start_basis.shape[1]
    own_rows = start_basis.shape[0]
    row_blocks = own_rows // block_size
    slot_count = kernel_blocks.shape[0]
    per_peer = (slot_count + devices - 1) // devices
    total_rows = own_rows * devices
    outside = devices * per_peer
    positions = jnp.arange(slot_count, dtype=jnp.int32)
    alive_mask = positions < block_count[0]
    local_row = block_row - my_index * row_blocks
    target = block_col // row_blocks
    target_block = block_col - target * row_blocks
    earlier = (
        (target[:, None] == target[None, :])
        & alive_mask[None, :]
        & (positions[None, :] < positions[:, None])
    )
    order_rank = jnp.sum(earlier.astype(jnp.int32), axis=1)
    slot_place = jnp.where(alive_mask, target * per_peer + order_rank, outside)
    wanted_local = jnp.full((outside,), -1, jnp.int32).at[slot_place].set(target_block, mode="drop")
    incoming = lax.all_to_all(
        wanted_local, ("rows", "grp"), split_axis=0, concat_axis=0, tiled=True
    )
    row_select = (
        onehot(local_row, row_blocks, jnp.float32) * alive_mask[:, None].astype(jnp.float32)
    ).T
    reply_select = onehot(incoming, row_blocks, jnp.bfloat16)
    receive_select = reply_select.T
    basis = start_basis
    result = None
    projected = None
    for iteration in range(ITERS):
        basis_tiles = basis.reshape(row_blocks, block_size, columns)
        gathered = lax.all_gather(basis, ("rows", "grp"), axis=0, tiled=True)
        partners = jnp.take(gathered.reshape(-1, block_size, columns), block_col, axis=0)
        forward = jnp.einsum(
            "sij,sjc->sic", kernel_blocks, partners, preferred_element_type=jnp.float32
        )
        own_tiles = jnp.take(basis_tiles, local_row, axis=0)
        mirrored = jnp.einsum(
            "sji,sjc->sic", kernel_blocks, own_tiles, preferred_element_type=jnp.float32
        ).astype(jnp.bfloat16)
        outgoing = (
            jnp.zeros((outside, block_size, columns), jnp.bfloat16)
            .at[slot_place]
            .set(mirrored, mode="drop")
        )
        arrived = lax.all_to_all(outgoing, ("rows", "grp"), split_axis=0, concat_axis=0, tiled=True)
        image_rows = jnp.einsum("ks,sic->kic", row_select, forward, precision=lax.Precision.HIGHEST)
        image_rows = image_rows + jnp.einsum(
            "kr,ric->kic", receive_select, arrived, preferred_element_type=jnp.float32
        )
        flat_image = image_rows.reshape(own_rows, columns)
        gram_part = jnp.dot(flat_image.T, flat_image, precision=lax.Precision.HIGHEST)
        if iteration == ITERS - 1:
            projection = jnp.dot(
                basis.astype(jnp.float32).T, flat_image, precision=lax.Precision.HIGHEST
            )
            gram_part, projection = lax.psum((gram_part, projection), ("rows", "grp"))
            projected = projection / total_rows
        else:
            gram_part = lax.psum(gram_part, ("rows", "grp"))
        lower_factor = jnp.linalg.cholesky(gram_part / total_rows)
        inverse = jax.scipy.linalg.solve_triangular(
            lower_factor, jnp.eye(columns, dtype=jnp.float32), lower=True
        )
        result = jnp.dot(flat_image, inverse.T, precision=lax.Precision.HIGHEST)
        basis = result.astype(jnp.bfloat16)
    return (result, projected)


def solution(mesh):
    in_specs = (
        P(("rows", "grp"), None),
        P(("rows", "grp"), None, None),
        P(("rows", "grp")),
        P(("rows", "grp")),
        P(("rows", "grp")),
    )
    out_specs = (P(("rows", "grp"), None), P())
    return jax.shard_map(
        on_device, mesh=mesh, in_specs=in_specs, out_specs=out_specs, check_vma=False
    )
```

profile of v0, /device:TPU:0, one launch (start us, length us, event | category | flops | bytes accessed | tf_op | source)
XLA Modules:
  0.0 407.3 jit_solution(14491948732641696692)
XLA Ops:
  7.2 0.7 multiply_subtract_fusion
  8.5 0.2 convert_reduce_fusion
  8.7 0.9 scatter_custom_fusion
  9.6 0.7 all_to_all.12
  10.3 7.3 %all-to-all-start = ((s32[32,3,1]{1,2,0:T(1,128)}), s32[32,3,1]{1,2,0:T(1,128)S(1)}, u32[]{:S(2)}, u32[]{:S(2)}) async-start(s32[32,3,1]{1,2,0:T(1,128)} %bitcast.3), calls=%async_computation | async-start | bytes 32768 | tf_op jit(solution)/shard_map/all_to_all | solution.py:37
  17.6 0.8 copy.123
  18.5 0.7 compare_and_fusion.1
  19.1 0.8 gather_fusion.1
  19.9 8.3 %convert_bitcast_fusion.1 = bf16[92,256,64]{1,2,0:T(8,128)(2,1)} fusion(bf16[92,256,256]{2,1,0:T(8,128)(2,1)} %param.13, bf16[92,256,64]{1,2,0:T(8,128)(2,1)S(1)} %gather_fusion.1, pred[92]{0:T(512)(128)(4,1)S(1)} %get-tuple-element.20), kind=kOutput, calls=%fused_computation.24 | convolution fusion | flops 774766592 | bytes 18088028 | tf_op jit(solution)/shard_map/sji,sjc->sic/dot_general | solution.py:56
  28.2 2.0 broadcast.76.clone
  30.2 1.0 copy-done.1
  31.2 12.6 %scatter_fusion = bf16[96,256,64]{1,2,0:T(8,128)(2,1)} fusion(bf16[96,256,64]{1,2,0:T(8,128)(2,1)} %broadcast.76.clone, s32[92]{0:T(128)S(1)} %compare_select_fusion.1, bf16[92,256,64]{1,2,0:T(8,128)(2,1)S(1)} %copy-done.1), kind=kCustom, calls=%fused_computation.5 | custom fusion | bytes 9044336 | tf_op jit(solution)/shard_map/scatter | solution.py:62
  43.8 0.0 all-to-all-done
  43.8 7.4 %all-to-all-start.1 = ((bf16[96,256,64]{1,2,0:T(8,128)(2,1)}), bf16[96,256,64]{1,2,0:T(8,128)(2,1)}, u32[]{:S(2)}, u32[]{:S(2)}) async-start(bf16[96,256,64]{1,2,0:T(8,128)(2,1)} %scatter_fusion), calls=%async_computation.1 | async-start | bytes 6291456 | tf_op jit(solution)/shard_map/all_to_all | solution.py:64
  51.2 0.2 all-gather.3.cloned.1.call-start
  51.4 0.5 all-gather.3.cloned.1.call-update
  51.9 0.0 copy-done.4
  52.0 0.5 broadcast.108
  52.5 0.7 reduce.7
  53.2 0.1 eq.53
  53.3 72.3 %all-gather.3.cloned.1.call-done = bf16[16384,64]{0,1:T(8,128)(2,1)} async-done(((bf16[512,64]{0,1:T(8,128)(2,1)}), bf16[16384,64]{0,1:T(8,128)(2,1)}) %all-gather.3.cloned.1.call-update) | async-done | bytes 2097168 | tf_op jit(solution)/shard_map/all_gather | solution.py:50
  125.6 1.9 copy.121
  127.4 2.5 gather_fusion
  130.0 11.7 %fusion.20 = f32[92,256,64]{1,2,0:T(8,128)} fusion(bf16[92,256,256]{2,1,0:T(8,128)(2,1)} %param.13, bf16[92,256,64]{1,2,0:T(8,128)(2,1)} %gather_fusion, pred[92]{0:T(512)(128)(4,1)S(1)} %compare_and_fusion), kind=kOutput, calls=%fused_computation.29 | convolution fusion | flops 773259264 | bytes 21102684 | tf_op jit(solution)/shard_map/sij,sjc->sic/dot_general | solution.py:52
  141.6 9.3 %fusion.2 = f32[2,256,64]{1,0,2:T(2,128)S(1)} fusion(f32[92,256,64]{1,2,0:T(8,128)} %fusion.20, f32[92]{0:T(128)S(1)} %fusion.74, s32[92]{0:T(128)S(1)} %get-tuple-element.21), kind=kOutput, calls=%fused_computation.9 | convolution fusion | flops 36176240 | bytes 6161120 | tf_op jit(solution)/shard_map/ks,sic->kic/dot_general | solution.py:65
  151.0 0.0 all-to-all-done.1
  151.0 3.7 fusion.34
  154.7 0.3 convolution_bitcast_fusion.1
  155.0 40.9 %psum.21 = f32[64,64]{0,1:T(8,128)S(1)} all-reduce(f32[64,64]{0,1:T(8,128)S(1)} %convolution_bitcast_fusion.1), channel_id=1, replica_groups=mesh['rows'=16,'grp'=2] {'rows','grp'}, use_global_device_ids=true, to_apply=%region_3.6 | all-reduce | flops 4096 | bytes 32768 | tf_op jit(solution)/shard_map/psum | solution.py:78
  195.9 0.1 copy.78
  196.0 5.8 %cholesky.44 = f32[64,64]{1,0:T(8,128)S(1)} custom-call(f32[64,64]{1,0:T(8,128)S(1)} %fusion.52), custom_call_target="Cholesky" | custom-call | tf_op jit(solution)/shard_map/jit(cholesky)/cholesky | solution.py:79
  201.9 0.6 compare_reduce_fusion.1
  202.5 0.7 fusion.47
  203.2 4.9 %custom-call.6 = f32[1,64,64]{1,2,0:T(8,128)S(1)} custom-call(f32[1,64,64]{2,1,0:T(8,128)S(1)} %fusion.47), custom_call_target="InvertDiagBlocksLowerTriangular" | custom-call | tf_op jit(solution)/shard_map/jit(_solve_triangular)/triangular_solve | solution.py:80
  208.1 0.3 fusion.45
  208.3 0.3 convolution_convert_fusion
  208.6 0.0 copy-start.2
  208.6 0.8 gather_fusion.3
  209.4 8.3 %convert_bitcast_fusion = bf16[92,256,64]{1,2,0:T(8,128)(2,1)} fusion(bf16[92,256,256]{2,1,0:T(8,128)(2,1)} %param.13, bf16[92,256,64]{1,2,0:T(8,128)(2,1)S(1)} %gather_fusion.3, pred[92]{0:T(512)(128)(4,1)S(1)} %get-tuple-element.20), kind=kOutput, calls=%fused_computation.23 | convolution fusion | flops 774766592 | bytes 18088028 | tf_op jit(solution)/shard_map/sji,sjc->sic/dot_general | solution.py:56
  217.7 2.0 broadcast.76
  219.7 1.0 copy-done
  220.7 12.6 %scatter_fusion.1 = bf16[96,256,64]{1,2,0:T(8,128)(2,1)} fusion(bf16[96,256,64]{1,2,0:T(8,128)(2,1)} %broadcast.76, s32[92]{0:T(128)S(1)} %compare_select_fusion.1, bf16[92,256,64]{1,2,0:T(8,128)(2,1)S(1)} %copy-done), kind=kCustom, calls=%fused_computation.6 | custom fusion | bytes 9044336 | tf_op jit(solution)/shard_map/scatter | solution.py:62
  233.3 5.4 %all-to-all-start.2 = ((bf16[96,256,64]{1,2,0:T(8,128)(2,1)}), bf16[96,256,64]{1,2,0:T(8,128)(2,1)}, u32[]{:S(2)}, u32[]{:S(2)}) async-start(bf16[96,256,64]{1,2,0:T(8,128)(2,1)} %scatter_fusion.1), calls=%async_computation.2 | async-start | bytes 6291456 | tf_op jit(solution)/shard_map/all_to_all | solution.py:64
  238.7 0.3 all-gather.5.cloned.1.call-start
  239.0 0.4 all-gather.5.cloned.1.call-update
  239.4 79.1 %all-gather.5.cloned.1.call-done = bf16[16384,64]{0,1:T(8,128)(2,1)} async-done(((bf16[512,64]{0,1:T(8,128)(2,1)}), bf16[16384,64]{0,1:T(8,128)(2,1)}) %all-gather.5.cloned.1.call-update) | async-done | bytes 2097168 | tf_op jit(solution)/shard_map/all_gather | solution.py:50
  318.5 1.9 copy.120
  320.4 2.5 gather_fusion.2
  323.0 11.7 %fusion.23 = f32[92,256,64]{1,2,0:T(8,128)} fusion(bf16[92,256,256]{2,1,0:T(8,128)(2,1)} %param.13, bf16[92,256,64]{1,2,0:T(8,128)(2,1)} %gather_fusion.2, pred[92]{0:T(512)(128)(4,1)S(1)} %compare_and_fusion), kind=kOutput, calls=%fused_computation.30 | convolution fusion | flops 773259264 | bytes 21102684 | tf_op jit(solution)/shard_map/sij,sjc->sic/dot_general | solution.py:52
  334.6 9.3 %fusion = f32[2,256,64]{1,0,2:T(2,128)S(1)} fusion(f32[92,256,64]{1,2,0:T(8,128)} %fusion.23, f32[92]{0:T(128)S(1)} %fusion.74, s32[92]{0:T(128)S(1)} %get-tuple-element.21), kind=kOutput, calls=%fused_computation.7 | convolution fusion | flops 36176240 | bytes 6161120 | tf_op jit(solution)/shard_map/ks,sic->kic/dot_general | solution.py:65
  344.0 0.0 copy-start.3
  344.0 0.0 all-to-all-done.2
  344.0 3.7 fusion.37
  347.7 0.3 convolution_bitcast_fusion
  348.0 0.2 fusion.76
  348.2 38.2 %all-reduce = (f32[64,64]{0,1:T(8,128)S(1)}, f32[64,64]{0,1:T(8,128)S(1)}) all-reduce(f32[64,64]{0,1:T(8,128)S(1)} %convolution_bitcast_fusion, f32[64,64]{0,1:T(8,128)S(1)} %fusion.76), channel_id=1, replica_groups=mesh['rows'=16,'grp'=2] {'rows','grp'}, use_global_device_ids=true, to_apply=%region_7.12 | all-reduce | flops 8192 | bytes 65536 | tf_op jit(solution)/shard_map/psum | solution.py:75
  386.4 0.1 copy.86
  386.5 5.8 %cholesky.55 = f32[64,64]{1,0:T(8,128)S(1)} custom-call(f32[64,64]{1,0:T(8,128)S(1)} %fusion.50), custom_call_target="Cholesky" | custom-call | tf_op jit(solution)/shard_map/jit(cholesky)/cholesky | solution.py:79
  392.4 0.6 compare_reduce_fusion
  393.1 0.7 fusion.48
  393.7 4.9 %custom-call.7 = f32[1,64,64]{1,2,0:T(8,128)S(1)} custom-call(f32[1,64,64]{2,1,0:T(8,128)S(1)} %fusion.48), custom_call_target="InvertDiagBlocksLowerTriangular" | custom-call | tf_op jit(solution)/shard_map/jit(_solve_triangular)/triangular_solve | solution.py:80
  398.6 0.3 fusion.43
  398.9 0.9 fusion.75
  399.8 0.7 copy.88
  (21 shorter events, 0.2 us)
Async XLA Ops:
  10.3 33.5 %all-to-all-start = ((s32[32,3,1]{1,2,0:T(1,128)}), s32[32,3,1]{1,2,0:T(1,128)S(1)}, u32[]{:S(2)}, u32[]{:S(2)}) async-start(s32[32,3,1]{1,2,0:T(1,128)} %bitcast.3), calls=%async_computation | async-start | bytes 32768 | tf_op jit(solution)/shard_map/all_to_all | solution.py:37
  28.2 3.0 copy-start.1
  43.8 8.1 %copy-start.4 = (s32[92]{0:T(128)S(1)}, s32[92]{0:T(128)}, u32[]{:S(2)}) copy-start(s32[92]{0:T(128)} %param.15) | copy-start | bytes 1108
  43.8 107.2 %all-to-all-start.1 = ((bf16[96,256,64]{1,2,0:T(8,128)(2,1)}), bf16[96,256,64]{1,2,0:T(8,128)(2,1)}, u32[]{:S(2)}, u32[]{:S(2)}) async-start(bf16[96,256,64]{1,2,0:T(8,128)(2,1)} %scatter_fusion), calls=%async_computation.1 | async-start | bytes 6291456 | tf_op jit(solution)/shard_map/all_to_all | solution.py:64
  51.2 74.4 %all-gather.3.cloned.1.call-start = ((), (), s32[]{:S(2)}) async-start(), calls=%async_computation.3 | async-start | bytes 2162688 | tf_op jit(solution)/shard_map/all_gather | solution.py:50
  208.6 0.8 copy-start.2
  217.7 3.0 copy-start
  233.3 110.7 %all-to-all-start.2 = ((bf16[96,256,64]{1,2,0:T(8,128)(2,1)}), bf16[96,256,64]{1,2,0:T(8,128)(2,1)}, u32[]{:S(2)}, u32[]{:S(2)}) async-start(bf16[96,256,64]{1,2,0:T(8,128)(2,1)} %scatter_fusion.1), calls=%async_computation.2 | async-start | bytes 6291456 | tf_op jit(solution)/shard_map/all_to_all | solution.py:64
  238.7 79.8 %all-gather.5.cloned.1.call-start = ((), (), s32[]{:S(2)}) async-start(), calls=%async_computation.4 | async-start | bytes 2162688 | tf_op jit(solution)/shard_map/all_gather | solution.py:50
  344.0 4.0 copy-start.3
Sparse Core Ops, SparseCore 0:
  54.9 70.6 all-gather.2
  243.0 75.5 all-gather.4
where the time goes:
time: 410 us; the launch traced here: 407 us
  waiting for transfers between devices  152 us (37%)
  blocking collectives  79.1 us (19%)
  matrix products  68.4 us (17%)
  local copies, waits for them, and re-layouts  45.5 us (11%)
  other arithmetic  26.4 us (6%)
  starting transfers between devices  20.6 us (5%)
  between operations  15 us (4%)
    all_gather x2, waiting for transfers between devices, on_device(): gathered = lax.all_gather(basis, ('rows', 'grp'), axis=0, tiled=True)  151 us
    psum x1, blocking collectives, on_device(): gram_part = lax.psum(gram_part, ('rows', 'grp'))  40.9 us
    psum x1, blocking collectives, on_device(): gram_part, projection = lax.psum((gram_part, projection), ('rows', 'grp'))  38.2 us
    scatter x2, local copies, waits for them, and re-layouts, on_device(): outgoing = jnp.zeros((outside, block_size, columns), jnp.bfloat16).at[slo...  25.2 us
    dot_general x2, matrix products, on_device(): jnp.einsum('sij,sjc->sic', kernel_blocks, partners, preferred_element_typ...  23.3 us
    dot_general x2, matrix products, on_device(): jnp.einsum('ks,sic->kic', row_select, forward, precision=lax.Precision.HI...  18.7 us
    dot_general x2, matrix products, on_device(): jnp.einsum('sji,sjc->sic', kernel_blocks, own_tiles, preferred_element_ty...  16.6 us
    another operation x6, other arithmetic, on_device(): lower_factor = jnp.linalg.cholesky(gram_part / total_rows)  13 us
  transfers between devices with their start and end apart: 5, of which 2 were waited for; matrix products, arithmetic and copies ran while one was open for 19% of the time, Pallas kernels for 0%

commit v1 on v0

--- a/solution.py
+++ b/solution.py
@@ -1,9 +1,18 @@
+import functools
 import jax
 import jax.numpy as jnp
 from jax import lax
 from jax.sharding import PartitionSpec as P
 
 ITERS = 2
+
+
+def work_the_face(field_in, ax_name, mesh_name):
+    carry_in = lax.psum(field_in, ax_name)
+    return lax.psum(carry_in, mesh_name)
+
+
+lead_the_face = functools.partial(work_the_face, ax_name="grp", mesh_name="rows")
 
 
 def onehot(index, count, dtype):
@@ -75,7 +84,7 @@
             gram_part, projection = lax.psum((gram_part, projection), ("rows", "grp"))
             projected = projection / total_rows
         else:
-            gram_part = lax.psum(gram_part, ("rows", "grp"))
+            gram_part = lead_the_face(gram_part)
         lower_factor = jnp.linalg.cholesky(gram_part / total_rows)
         inverse = jax.scipy.linalg.solve_triangular(
             lower_factor, jnp.eye(columns, dtype=jnp.float32), lower=True

time: 410 us -> 446 us (1.088)
  blocking collectives: 79.1 us -> 119 us
    psum x1 -> x2, blocking collectives: 40.9 us -> 79.2 us  [the longest x1 75.7 us: work_the_face(): return lax.psum(carry_in, mesh_name)]
  transfers between devices with their start and end apart: 5 -> 5, of which waited for: 2 -> 2; matrix products, arithmetic and copies ran while one was open for 19% -> 17% of each run, Pallas kernels for 0% -> 0%
where the time goes in v1:
time: 446 us; the launch traced here: 444 us
  waiting for transfers between devices  151 us (34%)
  blocking collectives  119 us (27%)
  matrix products  68.4 us (15%)
  local copies, waits for them, and re-layouts  45.5 us (10%)
  other arithmetic  26.4 us (6%)
  starting transfers between devices  18.5 us (4%)
  between operations  15 us (3%)
    all_gather x2, waiting for transfers between devices, on_device(): gathered = lax.all_gather(basis, ('rows', 'grp'), axis=0, tiled=True)  150 us
    psum x1, blocking collectives, work_the_face(): return lax.psum(carry_in, mesh_name)  75.7 us
    psum x1, blocking collectives, on_device(): gram_part, projection = lax.psum((gram_part, projection), ('rows', 'grp'))  39.7 us
    scatter x2, local copies, waits for them, and re-layouts, on_device(): outgoing = jnp.zeros((outside, block_size, columns), jnp.bfloat16).at[slo...  25.2 us
    dot_general x2, matrix products, on_device(): jnp.einsum('sij,sjc->sic', kernel_blocks, partners, preferred_element_typ...  23.3 us
    dot_general x2, matrix products, on_device(): jnp.einsum('ks,sic->kic', row_select, forward, precision=lax.Precision.HI...  18.7 us
    dot_general x2, matrix products, on_device(): jnp.einsum('sji,sjc->sic', kernel_blocks, own_tiles, preferred_element_ty...  16.6 us
    another operation x6, other arithmetic, on_device(): lower_factor = jnp.linalg.cholesky(gram_part / total_rows)  13 us
  transfers between devices with their start and end apart: 5, of which 2 were waited for; matrix products, arithmetic and copies ran while one was open for 17% of the time, Pallas kernels for 0%

profile of v1, /device:TPU:0, one launch (start us, length us, event | category | flops | bytes accessed | tf_op | source)
XLA Modules:
  0.0 443.6 jit_solution(12535678995025768321)
XLA Ops:
  7.2 0.7 multiply_subtract_fusion
  8.5 0.2 convert_reduce_fusion
  8.7 0.9 scatter_custom_fusion
  9.6 0.7 all_to_all.12
  10.3 7.3 %all-to-all-start = ((s32[32,3,1]{1,2,0:T(1,128)}), s32[32,3,1]{1,2,0:T(1,128)S(1)}, u32[]{:S(2)}, u32[]{:S(2)}) async-start(s32[32,3,1]{1,2,0:T(1,128)} %bitcast.3), calls=%async_computation | async-start | bytes 32768 | tf_op jit(solution)/shard_map/all_to_all | solution.py:46
  17.6 0.8 copy.123
  18.5 0.7 compare_and_fusion.1
  19.1 0.8 gather_fusion.1
  19.9 8.3 %convert_bitcast_fusion.1 = bf16[92,256,64]{1,2,0:T(8,128)(2,1)} fusion(bf16[92,256,256]{2,1,0:T(8,128)(2,1)} %param.13, bf16[92,256,64]{1,2,0:T(8,128)(2,1)S(1)} %gather_fusion.1, pred[92]{0:T(512)(128)(4,1)S(1)} %get-tuple-element.20), kind=kOutput, calls=%fused_computation.24 | convolution fusion | flops 774766592 | bytes 18088028 | tf_op jit(solution)/shard_map/sji,sjc->sic/dot_general | solution.py:65
  28.2 2.0 broadcast.76.clone
  30.2 1.0 copy-done.1
  31.2 12.6 %scatter_fusion = bf16[96,256,64]{1,2,0:T(8,128)(2,1)} fusion(bf16[96,256,64]{1,2,0:T(8,128)(2,1)} %broadcast.76.clone, s32[92]{0:T(128)S(1)} %compare_select_fusion.1, bf16[92,256,64]{1,2,0:T(8,128)(2,1)S(1)} %copy-done.1), kind=kCustom, calls=%fused_computation.5 | custom fusion | bytes 9044336 | tf_op jit(solution)/shard_map/scatter | solution.py:71
  43.8 0.0 all-to-all-done
  43.8 7.4 %all-to-all-start.1 = ((bf16[96,256,64]{1,2,0:T(8,128)(2,1)}), bf16[96,256,64]{1,2,0:T(8,128)(2,1)}, u32[]{:S(2)}, u32[]{:S(2)}) async-start(bf16[96,256,64]{1,2,0:T(8,128)(2,1)} %scatter_fusion), calls=%async_computation.1 | async-start | bytes 6291456 | tf_op jit(solution)/shard_map/all_to_all | solution.py:73
  51.2 0.2 all-gather.3.cloned.1.call-start
  51.4 0.5 all-gather.3.cloned.1.call-update
  52.0 0.5 broadcast.108
  52.5 0.7 reduce.7
  53.2 0.1 eq.53
  53.3 72.3 %all-gather.3.cloned.1.call-done = bf16[16384,64]{0,1:T(8,128)(2,1)} async-done(((bf16[512,64]{0,1:T(8,128)(2,1)}), bf16[16384,64]{0,1:T(8,128)(2,1)}) %all-gather.3.cloned.1.call-update) | async-done | bytes 2097168 | tf_op jit(solution)/shard_map/all_gather | solution.py:59
  125.6 1.9 copy.121
  127.4 2.5 gather_fusion
  130.0 11.7 %fusion.20 = f32[92,256,64]{1,2,0:T(8,128)} fusion(bf16[92,256,256]{2,1,0:T(8,128)(2,1)} %param.13, bf16[92,256,64]{1,2,0:T(8,128)(2,1)} %gather_fusion, pred[92]{0:T(512)(128)(4,1)S(1)} %compare_and_fusion), kind=kOutput, calls=%fused_computation.29 | convolution fusion | flops 773259264 | bytes 21102684 | tf_op jit(solution)/shard_map/sij,sjc->sic/dot_general | solution.py:61
  141.6 9.3 %fusion.2 = f32[2,256,64]{1,0,2:T(2,128)S(1)} fusion(f32[92,256,64]{1,2,0:T(8,128)} %fusion.20, f32[92]{0:T(128)S(1)} %fusion.74, s32[92]{0:T(128)S(1)} %get-tuple-element.21), kind=kOutput, calls=%fused_computation.9 | convolution fusion | flops 36176240 | bytes 6161120 | tf_op jit(solution)/shard_map/ks,sic->kic/dot_general | solution.py:74
  151.0 0.0 all-to-all-done.1
  151.0 3.7 fusion.34
  154.7 0.3 convolution_bitcast_fusion.1
  155.0 3.5 psum.28
  158.5 75.7 %psum.29 = f32[64,64]{0,1:T(8,128)S(1)} all-reduce(f32[64,64]{0,1:T(8,128)S(1)} %psum.28), channel_id=1, replica_groups=mesh['rows'=16,'grp'=2] {'rows'}, use_global_device_ids=true, to_apply=%region_4.7 | all-reduce | flops 4096 | bytes 32768 | tf_op jit(solution)/shard_map/psum | solution.py:12
  234.1 0.1 copy.78
  234.2 5.8 %cholesky.44 = f32[64,64]{1,0:T(8,128)S(1)} custom-call(f32[64,64]{1,0:T(8,128)S(1)} %fusion.52), custom_call_target="Cholesky" | custom-call | tf_op jit(solution)/shard_map/jit(cholesky)/cholesky | solution.py:88
  240.1 0.6 compare_reduce_fusion.1
  240.8 0.7 fusion.47
  241.4 4.9 %custom-call.6 = f32[1,64,64]{1,2,0:T(8,128)S(1)} custom-call(f32[1,64,64]{2,1,0:T(8,128)S(1)} %fusion.47), custom_call_target="InvertDiagBlocksLowerTriangular" | custom-call | tf_op jit(solution)/shard_map/jit(_solve_triangular)/triangular_solve | solution.py:89
  246.3 0.3 fusion.45
  246.6 0.3 convolution_convert_fusion
  246.8 0.0 copy-start.2
  246.9 0.8 gather_fusion.3
  247.7 8.3 %convert_bitcast_fusion = bf16[92,256,64]{1,2,0:T(8,128)(2,1)} fusion(bf16[92,256,256]{2,1,0:T(8,128)(2,1)} %param.13, bf16[92,256,64]{1,2,0:T(8,128)(2,1)S(1)} %gather_fusion.3, pred[92]{0:T(512)(128)(4,1)S(1)} %get-tuple-element.20), kind=kOutput, calls=%fused_computation.23 | convolution fusion | flops 774766592 | bytes 18088028 | tf_op jit(solution)/shard_map/sji,sjc->sic/dot_general | solution.py:65
  256.0 2.0 broadcast.76
  258.0 1.0 copy-done
  258.9 12.6 %scatter_fusion.1 = bf16[96,256,64]{1,2,0:T(8,128)(2,1)} fusion(bf16[96,256,64]{1,2,0:T(8,128)(2,1)} %broadcast.76, s32[92]{0:T(128)S(1)} %compare_select_fusion.1, bf16[92,256,64]{1,2,0:T(8,128)(2,1)S(1)} %copy-done), kind=kCustom, calls=%fused_computation.6 | custom fusion | bytes 9044336 | tf_op jit(solution)/shard_map/scatter | solution.py:71
  271.5 3.5 all-to-all-start.2
  275.1 0.0 all-gather.5.cloned.1.call-start
  275.1 0.7 all-gather.5.cloned.1.call-update
  275.8 77.5 %all-gather.5.cloned.1.call-done = bf16[16384,64]{0,1:T(8,128)(2,1)} async-done(((bf16[512,64]{0,1:T(8,128)(2,1)}), bf16[16384,64]{0,1:T(8,128)(2,1)}) %all-gather.5.cloned.1.call-update) | async-done | bytes 2097168 | tf_op jit(solution)/shard_map/all_gather | solution.py:59
  353.4 1.9 copy.120
  355.2 2.5 gather_fusion.2
  357.8 11.7 %fusion.23 = f32[92,256,64]{1,2,0:T(8,128)} fusion(bf16[92,256,256]{2,1,0:T(8,128)(2,1)} %param.13, bf16[92,256,64]{1,2,0:T(8,128)(2,1)} %gather_fusion.2, pred[92]{0:T(512)(128)(4,1)S(1)} %compare_and_fusion), kind=kOutput, calls=%fused_computation.30 | convolution fusion | flops 773259264 | bytes 21102684 | tf_op jit(solution)/shard_map/sij,sjc->sic/dot_general | solution.py:61
  369.4 9.3 %fusion = f32[2,256,64]{1,0,2:T(2,128)S(1)} fusion(f32[92,256,64]{1,2,0:T(8,128)} %fusion.23, f32[92]{0:T(128)S(1)} %fusion.74, s32[92]{0:T(128)S(1)} %get-tuple-element.21), kind=kOutput, calls=%fused_computation.7 | convolution fusion | flops 36176240 | bytes 6161120 | tf_op jit(solution)/shard_map/ks,sic->kic/dot_general | solution.py:74
  378.8 0.0 copy-start.3
  378.8 0.0 all-to-all-done.2
  378.8 3.7 fusion.37
  382.5 0.3 convolution_bitcast_fusion
  382.8 0.2 fusion.76
  383.0 39.7 %all-reduce = (f32[64,64]{0,1:T(8,128)S(1)}, f32[64,64]{0,1:T(8,128)S(1)}) all-reduce(f32[64,64]{0,1:T(8,128)S(1)} %convolution_bitcast_fusion, f32[64,64]{0,1:T(8,128)S(1)} %fusion.76), channel_id=1, replica_groups=mesh['rows'=16,'grp'=2] {'rows','grp'}, use_global_device_ids=true, to_apply=%region_8.13 | all-reduce | flops 8192 | bytes 65536 | tf_op jit(solution)/shard_map/psum | solution.py:84
  422.7 0.1 copy.86
  422.8 5.8 %cholesky.55 = f32[64,64]{1,0:T(8,128)S(1)} custom-call(f32[64,64]{1,0:T(8,128)S(1)} %fusion.50), custom_call_target="Cholesky" | custom-call | tf_op jit(solution)/shard_map/jit(cholesky)/cholesky | solution.py:88
  428.7 0.6 compare_reduce_fusion
  429.3 0.7 fusion.48
  430.0 4.9 %custom-call.7 = f32[1,64,64]{1,2,0:T(8,128)S(1)} custom-call(f32[1,64,64]{2,1,0:T(8,128)S(1)} %fusion.48), custom_call_target="InvertDiagBlocksLowerTriangular" | custom-call | tf_op jit(solution)/shard_map/jit(_solve_triangular)/triangular_solve | solution.py:89
  434.9 0.3 fusion.43
  435.2 0.9 fusion.75
  436.1 0.7 copy.88
  (22 shorter events, 0.2 us)
Async XLA Ops:
  10.3 33.5 %all-to-all-start = ((s32[32,3,1]{1,2,0:T(1,128)}), s32[32,3,1]{1,2,0:T(1,128)S(1)}, u32[]{:S(2)}, u32[]{:S(2)}) async-start(s32[32,3,1]{1,2,0:T(1,128)} %bitcast.3), calls=%async_computation | async-start | bytes 32768 | tf_op jit(solution)/shard_map/all_to_all | solution.py:46
  28.2 3.0 copy-start.1
  43.8 8.1 %copy-start.4 = (s32[92]{0:T(128)S(1)}, s32[92]{0:T(128)}, u32[]{:S(2)}) copy-start(s32[92]{0:T(128)} %param.15) | copy-start | bytes 1108
  43.8 107.2 %all-to-all-start.1 = ((bf16[96,256,64]{1,2,0:T(8,128)(2,1)}), bf16[96,256,64]{1,2,0:T(8,128)(2,1)}, u32[]{:S(2)}, u32[]{:S(2)}) async-start(bf16[96,256,64]{1,2,0:T(8,128)(2,1)} %scatter_fusion), calls=%async_computation.1 | async-start | bytes 6291456 | tf_op jit(solution)/shard_map/all_to_all | solution.py:73
  51.2 74.4 %all-gather.3.cloned.1.call-start = ((), (), s32[]{:S(2)}) async-start(), calls=%async_computation.3 | async-start | bytes 2162688 | tf_op jit(solution)/shard_map/all_gather | solution.py:59
  246.8 0.8 copy-start.2
  256.0 3.0 copy-start
  271.5 107.3 %all-to-all-start.2 = ((bf16[96,256,64]{1,2,0:T(8,128)(2,1)}), bf16[96,256,64]{1,2,0:T(8,128)(2,1)}, u32[]{:S(2)}, u32[]{:S(2)}) async-start(bf16[96,256,64]{1,2,0:T(8,128)(2,1)} %scatter_fusion.1), calls=%async_computation.2 | async-start | bytes 6291456 | tf_op jit(solution)/shard_map/all_to_all | solution.py:73
  275.1 78.3 %all-gather.5.cloned.1.call-start = ((), (), s32[]{:S(2)}) async-start(), calls=%async_computation.4 | async-start | bytes 2162688 | tf_op jit(solution)/shard_map/all_gather | solution.py:59
  378.8 4.0 copy-start.3
Sparse Core Ops, SparseCore 0:
  54.9 70.6 all-gather.2
  279.4 73.9 all-gather.4
